TPU v7x, 256 devices: a whole 4x4x8 slice. The times are simulated.
256 devices in a mesh: blk: 16 (over z, core), segment: 2 (over y_hi), rep: 8 (over x, y_lo).
Axes of the slice: x: 4, y: 4 (y_hi: 2, y_lo: 2; y = y_hi * 2 + y_lo), z: 8, core: 2. Of those that a mesh axis runs over, the one named last changes fastest.
Arguments:
- features: bfloat16 [16384, 256], P('blk'), may hold values from -14 to 14
- tile_weight: bfloat16 [49152, 128, 128], P(('blk', 'segment', 'rep')), may hold values from -0.099609375 to 0.099609375
- tile_limit: int32 [49152, 128], P(('blk', 'segment', 'rep')), may hold values from 1 to 128
- tile_src: int32 [49152, 1], P(('blk', 'segment', 'rep')), may hold values from 0 to 15; in each aligned block of 192 rows (0 to 191, 192 to 383, ...) at most 24 rows name the same one
- tile_row: int32 [49152], P(('blk', 'segment', 'rep')), may hold values from 0 to 5
- tile_col: int32 [49152], P(('blk', 'segment', 'rep')), may hold values from 0 to 7
- gain_one: float32 [256], replicated, may hold values from 0.25 to 1.75
- up_one: bfloat16 [256, 1024], replicated, may hold values from -0.375 to 0.375
- down_one: bfloat16 [1024, 256], replicated, may hold values from -0.25 to 0.25
- gain_two: float32 [256], replicated, may hold values from 0.25 to 1.75
- gate_two: bfloat16 [256, 2048], P(None, ('segment', 'rep')), may hold values from -0.375 to 0.375
- up_two: bfloat16 [256, 2048], P(None, ('segment', 'rep')), may hold values from -0.375 to 0.375
- down_two: bfloat16 [256, 2048], P(None, ('segment', 'rep')), may hold values from -0.25 to 0.25
Outputs:
- readout: bfloat16 [196608, 256], P(('blk', 'segment', 'rep'))
Inputs may be any that keep to these rules, and one draw needn't show every extreme that they name: `tile_src`: among the 192 tiles of one device at most 24 name the same partition, a bound that some block reaches.
All inputs are finite; a program needn't handle non-finite values.
Results may differ from a plain program's by a relative error of at most 0.0062.
Values may be sent and summed in bfloat16 or wider, within the bound.
No kernel may reach another device: no remote copies, remote signals or barrier semaphores. Data moves between devices by JAX's collectives and lax.ppermute only.
A program may use at most 128 MiB of HBM per device.

v0:
```python
import jax
import jax.numpy as jnp
from jax import lax
from jax.sharding import PartitionSpec as P

FEATURES = 256
TILE_SIZE = 128
SRC_BLOCK = 1024
DEST_DEV = 768
TILE_COUNT = 192
SLOT_CAP = 24


def rms_scaled(values, norm_gain):
    mean_square = jnp.mean(values * values, axis=-1, keepdims=True)
    return values * lax.rsqrt(mean_square + 1e-06) * norm_gain


def local(
    features,
    tile_weight,
    tile_limit,
    tile_src,
    tile_row,
    tile_col,
    gain_one,
    up_one,
    down_one,
    gain_two,
    gate_two,
    up_two,
    down_two,
):
    row_tiles = DEST_DEV // TILE_SIZE
    col_tiles = SRC_BLOCK // TILE_SIZE
    columns = jnp.arange(TILE_SIZE, dtype=jnp.int32)
    row_ids = jnp.arange(row_tiles, dtype=jnp.int32)
    masked = jnp.where(
        columns[None, None, :] < tile_limit[:, :, None],
        tile_weight,
        jnp.zeros((), tile_weight.dtype),
    )
    sources = tile_src[:, 0]
    partitions = lax.axis_size("blk")
    part_ids = jnp.arange(partitions, dtype=jnp.int32)
    member = (sources[:, None] == part_ids[None, :]).astype(jnp.int32)
    rank_table = jnp.cumsum(member, axis=0) - 1
    rank_held = jnp.sum(rank_table * member, axis=1)
    slot_ids = jnp.arange(SLOT_CAP, dtype=jnp.int32)
    slot_match = member[:, :, None] * (rank_held[:, None, None] == slot_ids[None, None, :]).astype(
        jnp.int32
    )
    tile_ids = jnp.arange(TILE_COUNT, dtype=jnp.int32)
    slot_tile = jnp.sum(slot_match * tile_ids[:, None, None], axis=0)
    slot_live = jnp.sum(slot_match, axis=0).astype(jnp.float32)
    zero_rows = jnp.zeros((row_tiles, TILE_SIZE, FEATURES), jnp.float32)
    source_piece = lax.all_gather(features, "blk", axis=0, tiled=True)
    block_count = source_piece.shape[0] // SRC_BLOCK

    def one_block(block_step, running):
        chosen = lax.dynamic_index_in_dim(slot_tile, block_step, 0, keepdims=False)
        live_now = lax.dynamic_index_in_dim(slot_live, block_step, 0, keepdims=False)
        source_tiles = lax.dynamic_slice_in_dim(source_piece, block_step * SRC_BLOCK, SRC_BLOCK, 0)
        source_tiles = source_tiles.reshape(col_tiles, TILE_SIZE, FEATURES)
        picked = source_tiles[tile_col[chosen]]
        contrib = jnp.einsum(
            "sij,sjf->sif", masked[chosen], picked, preferred_element_type=jnp.float32
        )
        onehot = (tile_row[chosen][:, None] == row_ids[None, :]).astype(jnp.float32) * live_now[
            :, None
        ]
        return running + jnp.einsum("sr,sif->rif", onehot, contrib, precision=lax.Precision.HIGHEST)

    summed = lax.fori_loop(0, block_count, one_block, zero_rows)
    aggregated = summed.reshape(DEST_DEV, FEATURES)
    normed_one = rms_scaled(aggregated, gain_one).astype(jnp.bfloat16)
    hidden_one = jnp.maximum(
        jnp.dot(normed_one, up_one, preferred_element_type=jnp.float32), 0.0
    ).astype(jnp.bfloat16)
    section_one = aggregated + jnp.dot(hidden_one, down_one, preferred_element_type=jnp.float32)
    normed_two = rms_scaled(section_one, gain_two).astype(jnp.bfloat16)
    gate_value = jnp.dot(
        normed_two,
        lax.all_gather(gate_two, ("segment", "rep"), axis=1, tiled=True),
        preferred_element_type=jnp.float32,
    )
    up_value = jnp.dot(
        normed_two,
        lax.all_gather(up_two, ("segment", "rep"), axis=1, tiled=True),
        preferred_element_type=jnp.float32,
    )
    hidden_two = (jax.nn.silu(gate_value) * up_value).astype(jnp.bfloat16)
    branch_two = lax.dot_general(
        hidden_two,
        lax.all_gather(down_two, ("segment", "rep"), axis=1, tiled=True),
        (((1,), (1,)), ((), ())),
        preferred_element_type=jnp.float32,
    )
    return (section_one + branch_two).astype(jnp.bfloat16)


def solution(mesh):
    in_specs = (
        P("blk", None),
        P(("blk", "segment", "rep"), None, None),
        P(("blk", "segment", "rep"), None),
        P(("blk", "segment", "rep"), None),
        P(("blk", "segment", "rep")),
        P(("blk", "segment", "rep")),
        P(),
        P(),
        P(),
        P(),
        P(None, ("segment", "rep")),
        P(None, ("segment", "rep")),
        P(None, ("segment", "rep")),
    )
    out_specs = P(("blk", "segment", "rep"), None)
    return jax.shard_map(local, mesh=mesh, in_specs=in_specs, out_specs=out_specs, check_vma=False)
```

profile of v0, /device:TPU:1, one launch (start us, length us, event | category | flops | bytes accessed | tf_op | source)
XLA Modules:
  0.0 340.6 jit_solution(471552748736940421)
XLA Ops:
  13.0 7.0 %fusion.17 = bf16[192,128,128]{2,1,0:T(8,128)(2,1)} fusion(bf16[192,128,128]{2,1,0:T(8,128)(2,1)} %param.16, s32[192,128]{1,0:T(8,128)} %param.17), kind=kLoop, calls=%fused_computation.27 | loop fusion | flops 6291456 | bytes 12681216 | tf_op jit(solution)/shard_map/jit(_where)/select_n | solution.py:38
  20.0 49.2 %all-gather.5.cloned.1.call-done = bf16[16384,256]{1,0:T(8,128)(2,1)} async-done(((bf16[1024,256]{1,0:T(8,128)(2,1)}), bf16[16384,256]{1,0:T(8,128)(2,1)}) %all-gather.5.cloned.1.call-update) | async-done | bytes 8388624 | tf_op jit(solution)/shard_map/all_gather | solution.py:57
  69.2 247.6 %while.14 = (s32[]{:T(128)}, f32[6,128,256]{2,0,1:T(8,128)}, s32[16,24]{1,0:T(8,128)S(1)}, s32[192]{0:T(256)S(1)}, f32[16,24]{1,0:T(8,128)S(1)}, /*index=5*/bf16...) while((s32[]{:T(128)}, f32[6,128,256]{2,0,1:T(8,128)}, ...), condition=%wide.region_6.7_spmd.clone, body=%wide.region_5.6_spmd.clone.sunk | while | flops 258345392 | bytes 16000889 | solution.py:74
  69.2 1.1 constant_dynamic-slice_fusion.4
  71.7 3.5 %gather_fusion = bf16[24,128,128]{2,1,0:T(8,128)(2,1)S(1)} fusion(bf16[192,128,128]{2,1,0:T(8,128)(2,1)} %get-tuple-element.287, s32[1024]{0:T(1024)S(1)} %pad_clamp_fusion.4), kind=kCustom, calls=%fused_computation.1.clone.clone.1 | custom fusion | bytes 1572960 | tf_op jit(solution)/shard_map/while/body/eval_jaxpr/gather | solution.py:67
  75.2 2.2 fusion.64
  78.1 6.3 %fusion.66 = f32[6,128,256]{2,0,1:T(8,128)} fusion(f32[24,128,256]{2,1,0:T(8,128)} %fusion.64, f32[6,128,256]{2,0,1:T(8,128)} %get-tuple-element.271, pred[]{:T(512)S(6)} %compare.4, f32[24]{0:T(128)S(1)} %fusion.65, s32[24]{0:T(128)S(1)} %gather_fusion.3), kind=kOutput, calls=%fused_computation.7.clone.1 | convolution fusion | flops 57016608 | bytes 4718785 | tf_op jit(solution)/shard_map/while/body/eval_jaxpr/sr,sif->rif/dot_general | solution.py:72
  84.5 1.1 constant_dynamic-slice_fusion.4
  86.9 3.5 %gather_fusion = bf16[24,128,128]{2,1,0:T(8,128)(2,1)S(1)} fusion(bf16[192,128,128]{2,1,0:T(8,128)(2,1)} %get-tuple-element.287, s32[1024]{0:T(1024)S(1)} %pad_clamp_fusion.4), kind=kCustom, calls=%fused_computation.1.clone.clone.1 | custom fusion | bytes 1572960 | tf_op jit(solution)/shard_map/while/body/eval_jaxpr/gather | solution.py:67
  90.4 2.2 fusion.64
  93.3 6.6 %fusion.66 = f32[6,128,256]{2,0,1:T(8,128)} fusion(f32[24,128,256]{2,1,0:T(8,128)} %fusion.64, f32[6,128,256]{2,0,1:T(8,128)} %get-tuple-element.271, pred[]{:T(512)S(6)} %compare.4, f32[24]{0:T(128)S(1)} %fusion.65, s32[24]{0:T(128)S(1)} %gather_fusion.3), kind=kOutput, calls=%fused_computation.7.clone.1 | convolution fusion | flops 57016608 | bytes 4718785 | tf_op jit(solution)/shard_map/while/body/eval_jaxpr/sr,sif->rif/dot_general | solution.py:72
  100.0 1.1 constant_dynamic-slice_fusion.4
  102.5 3.5 %gather_fusion = bf16[24,128,128]{2,1,0:T(8,128)(2,1)S(1)} fusion(bf16[192,128,128]{2,1,0:T(8,128)(2,1)} %get-tuple-element.287, s32[1024]{0:T(1024)S(1)} %pad_clamp_fusion.4), kind=kCustom, calls=%fused_computation.1.clone.clone.1 | custom fusion | bytes 1572960 | tf_op jit(solution)/shard_map/while/body/eval_jaxpr/gather | solution.py:67
  106.0 2.2 fusion.64
  108.9 6.6 %fusion.66 = f32[6,128,256]{2,0,1:T(8,128)} fusion(f32[24,128,256]{2,1,0:T(8,128)} %fusion.64, f32[6,128,256]{2,0,1:T(8,128)} %get-tuple-element.271, pred[]{:T(512)S(6)} %compare.4, f32[24]{0:T(128)S(1)} %fusion.65, s32[24]{0:T(128)S(1)} %gather_fusion.3), kind=kOutput, calls=%fused_computation.7.clone.1 | convolution fusion | flops 57016608 | bytes 4718785 | tf_op jit(solution)/shard_map/while/body/eval_jaxpr/sr,sif->rif/dot_general | solution.py:72
  115.5 1.1 constant_dynamic-slice_fusion.4
  118.0 3.5 %gather_fusion = bf16[24,128,128]{2,1,0:T(8,128)(2,1)S(1)} fusion(bf16[192,128,128]{2,1,0:T(8,128)(2,1)} %get-tuple-element.287, s32[1024]{0:T(1024)S(1)} %pad_clamp_fusion.4), kind=kCustom, calls=%fused_computation.1.clone.clone.1 | custom fusion | bytes 1572960 | tf_op jit(solution)/shard_map/while/body/eval_jaxpr/gather | solution.py:67
  121.5 2.2 fusion.64
  124.4 6.6 %fusion.66 = f32[6,128,256]{2,0,1:T(8,128)} fusion(f32[24,128,256]{2,1,0:T(8,128)} %fusion.64, f32[6,128,256]{2,0,1:T(8,128)} %get-tuple-element.271, pred[]{:T(512)S(6)} %compare.4, f32[24]{0:T(128)S(1)} %fusion.65, s32[24]{0:T(128)S(1)} %gather_fusion.3), kind=kOutput, calls=%fused_computation.7.clone.1 | convolution fusion | flops 57016608 | bytes 4718785 | tf_op jit(solution)/shard_map/while/body/eval_jaxpr/sr,sif->rif/dot_general | solution.py:72
  133.4 3.5 %gather_fusion = bf16[24,128,128]{2,1,0:T(8,128)(2,1)S(1)} fusion(bf16[192,128,128]{2,1,0:T(8,128)(2,1)} %get-tuple-element.287, s32[1024]{0:T(1024)S(1)} %pad_clamp_fusion.4), kind=kCustom, calls=%fused_computation.1.clone.clone.1 | custom fusion | bytes 1572960 | tf_op jit(solution)/shard_map/while/body/eval_jaxpr/gather | solution.py:67
  136.9 2.2 fusion.64
  139.8 6.6 %fusion.66 = f32[6,128,256]{2,0,1:T(8,128)} fusion(f32[24,128,256]{2,1,0:T(8,128)} %fusion.64, f32[6,128,256]{2,0,1:T(8,128)} %get-tuple-element.271, pred[]{:T(512)S(6)} %compare.4, f32[24]{0:T(128)S(1)} %fusion.65, s32[24]{0:T(128)S(1)} %gather_fusion.3), kind=kOutput, calls=%fused_computation.7.clone.1 | convolution fusion | flops 57016608 | bytes 4718785 | tf_op jit(solution)/shard_map/while/body/eval_jaxpr/sr,sif->rif/dot_general | solution.py:72
  148.9 3.5 %gather_fusion = bf16[24,128,128]{2,1,0:T(8,128)(2,1)S(1)} fusion(bf16[192,128,128]{2,1,0:T(8,128)(2,1)} %get-tuple-element.287, s32[1024]{0:T(1024)S(1)} %pad_clamp_fusion.4), kind=kCustom, calls=%fused_computation.1.clone.clone.1 | custom fusion | bytes 1572960 | tf_op jit(solution)/shard_map/while/body/eval_jaxpr/gather | solution.py:67
  152.4 2.2 fusion.64
  155.3 6.6 %fusion.66 = f32[6,128,256]{2,0,1:T(8,128)} fusion(f32[24,128,256]{2,1,0:T(8,128)} %fusion.64, f32[6,128,256]{2,0,1:T(8,128)} %get-tuple-element.271, pred[]{:T(512)S(6)} %compare.4, f32[24]{0:T(128)S(1)} %fusion.65, s32[24]{0:T(128)S(1)} %gather_fusion.3), kind=kOutput, calls=%fused_computation.7.clone.1 | convolution fusion | flops 57016608 | bytes 4718785 | tf_op jit(solution)/shard_map/while/body/eval_jaxpr/sr,sif->rif/dot_general | solution.py:72
  164.4 3.5 %gather_fusion = bf16[24,128,128]{2,1,0:T(8,128)(2,1)S(1)} fusion(bf16[192,128,128]{2,1,0:T(8,128)(2,1)} %get-tuple-element.287, s32[1024]{0:T(1024)S(1)} %pad_clamp_fusion.4), kind=kCustom, calls=%fused_computation.1.clone.clone.1 | custom fusion | bytes 1572960 | tf_op jit(solution)/shard_map/while/body/eval_jaxpr/gather | solution.py:67
  167.9 2.2 fusion.64
  170.9 6.6 %fusion.66 = f32[6,128,256]{2,0,1:T(8,128)} fusion(f32[24,128,256]{2,1,0:T(8,128)} %fusion.64, f32[6,128,256]{2,0,1:T(8,128)} %get-tuple-element.271, pred[]{:T(512)S(6)} %compare.4, f32[24]{0:T(128)S(1)} %fusion.65, s32[24]{0:T(128)S(1)} %gather_fusion.3), kind=kOutput, calls=%fused_computation.7.clone.1 | convolution fusion | flops 57016608 | bytes 4718785 | tf_op jit(solution)/shard_map/while/body/eval_jaxpr/sr,sif->rif/dot_general | solution.py:72
  179.9 3.5 %gather_fusion = bf16[24,128,128]{2,1,0:T(8,128)(2,1)S(1)} fusion(bf16[192,128,128]{2,1,0:T(8,128)(2,1)} %get-tuple-element.287, s32[1024]{0:T(1024)S(1)} %pad_clamp_fusion.4), kind=kCustom, calls=%fused_computation.1.clone.clone.1 | custom fusion | bytes 1572960 | tf_op jit(solution)/shard_map/while/body/eval_jaxpr/gather | solution.py:67
  183.4 2.2 fusion.64
  186.3 6.6 %fusion.66 = f32[6,128,256]{2,0,1:T(8,128)} fusion(f32[24,128,256]{2,1,0:T(8,128)} %fusion.64, f32[6,128,256]{2,0,1:T(8,128)} %get-tuple-element.271, pred[]{:T(512)S(6)} %compare.4, f32[24]{0:T(128)S(1)} %fusion.65, s32[24]{0:T(128)S(1)} %gather_fusion.3), kind=kOutput, calls=%fused_computation.7.clone.1 | convolution fusion | flops 57016608 | bytes 4718785 | tf_op jit(solution)/shard_map/while/body/eval_jaxpr/sr,sif->rif/dot_general | solution.py:72
  193.0 1.1 constant_dynamic-slice_fusion.4
  195.5 3.5 %gather_fusion = bf16[24,128,128]{2,1,0:T(8,128)(2,1)S(1)} fusion(bf16[192,128,128]{2,1,0:T(8,128)(2,1)} %get-tuple-element.287, s32[1024]{0:T(1024)S(1)} %pad_clamp_fusion.4), kind=kCustom, calls=%fused_computation.1.clone.clone.1 | custom fusion | bytes 1572960 | tf_op jit(solution)/shard_map/while/body/eval_jaxpr/gather | solution.py:67
  199.0 2.2 fusion.64
  201.9 6.6 %fusion.66 = f32[6,128,256]{2,0,1:T(8,128)} fusion(f32[24,128,256]{2,1,0:T(8,128)} %fusion.64, f32[6,128,256]{2,0,1:T(8,128)} %get-tuple-element.271, pred[]{:T(512)S(6)} %compare.4, f32[24]{0:T(128)S(1)} %fusion.65, s32[24]{0:T(128)S(1)} %gather_fusion.3), kind=kOutput, calls=%fused_computation.7.clone.1 | convolution fusion | flops 57016608 | bytes 4718785 | tf_op jit(solution)/shard_map/while/body/eval_jaxpr/sr,sif->rif/dot_general | solution.py:72
  210.9 3.5 %gather_fusion = bf16[24,128,128]{2,1,0:T(8,128)(2,1)S(1)} fusion(bf16[192,128,128]{2,1,0:T(8,128)(2,1)} %get-tuple-element.287, s32[1024]{0:T(1024)S(1)} %pad_clamp_fusion.4), kind=kCustom, calls=%fused_computation.1.clone.clone.1 | custom fusion | bytes 1572960 | tf_op jit(solution)/shard_map/while/body/eval_jaxpr/gather | solution.py:67
  214.4 2.2 fusion.64
  217.3 6.6 %fusion.66 = f32[6,128,256]{2,0,1:T(8,128)} fusion(f32[24,128,256]{2,1,0:T(8,128)} %fusion.64, f32[6,128,256]{2,0,1:T(8,128)} %get-tuple-element.271, pred[]{:T(512)S(6)} %compare.4, f32[24]{0:T(128)S(1)} %fusion.65, s32[24]{0:T(128)S(1)} %gather_fusion.3), kind=kOutput, calls=%fused_computation.7.clone.1 | convolution fusion | flops 57016608 | bytes 4718785 | tf_op jit(solution)/shard_map/while/body/eval_jaxpr/sr,sif->rif/dot_general | solution.py:72
  226.4 3.5 %gather_fusion = bf16[24,128,128]{2,1,0:T(8,128)(2,1)S(1)} fusion(bf16[192,128,128]{2,1,0:T(8,128)(2,1)} %get-tuple-element.287, s32[1024]{0:T(1024)S(1)} %pad_clamp_fusion.4), kind=kCustom, calls=%fused_computation.1.clone.clone.1 | custom fusion | bytes 1572960 | tf_op jit(solution)/shard_map/while/body/eval_jaxpr/gather | solution.py:67
  229.9 2.2 fusion.64
  232.8 6.6 %fusion.66 = f32[6,128,256]{2,0,1:T(8,128)} fusion(f32[24,128,256]{2,1,0:T(8,128)} %fusion.64, f32[6,128,256]{2,0,1:T(8,128)} %get-tuple-element.271, pred[]{:T(512)S(6)} %compare.4, f32[24]{0:T(128)S(1)} %fusion.65, s32[24]{0:T(128)S(1)} %gather_fusion.3), kind=kOutput, calls=%fused_computation.7.clone.1 | convolution fusion | flops 57016608 | bytes 4718785 | tf_op jit(solution)/shard_map/while/body/eval_jaxpr/sr,sif->rif/dot_general | solution.py:72
  239.4 1.1 constant_dynamic-slice_fusion.4
  241.9 3.5 %gather_fusion = bf16[24,128,128]{2,1,0:T(8,128)(2,1)S(1)} fusion(bf16[192,128,128]{2,1,0:T(8,128)(2,1)} %get-tuple-element.287, s32[1024]{0:T(1024)S(1)} %pad_clamp_fusion.4), kind=kCustom, calls=%fused_computation.1.clone.clone.1 | custom fusion | bytes 1572960 | tf_op jit(solution)/shard_map/while/body/eval_jaxpr/gather | solution.py:67
  245.4 2.2 fusion.64
  248.3 6.6 %fusion.66 = f32[6,128,256]{2,0,1:T(8,128)} fusion(f32[24,128,256]{2,1,0:T(8,128)} %fusion.64, f32[6,128,256]{2,0,1:T(8,128)} %get-tuple-element.271, pred[]{:T(512)S(6)} %compare.4, f32[24]{0:T(128)S(1)} %fusion.65, s32[24]{0:T(128)S(1)} %gather_fusion.3), kind=kOutput, calls=%fused_computation.7.clone.1 | convolution fusion | flops 57016608 | bytes 4718785 | tf_op jit(solution)/shard_map/while/body/eval_jaxpr/sr,sif->rif/dot_general | solution.py:72
  257.4 3.5 %gather_fusion = bf16[24,128,128]{2,1,0:T(8,128)(2,1)S(1)} fusion(bf16[192,128,128]{2,1,0:T(8,128)(2,1)} %get-tuple-element.287, s32[1024]{0:T(1024)S(1)} %pad_clamp_fusion.4), kind=kCustom, calls=%fused_computation.1.clone.clone.1 | custom fusion | bytes 1572960 | tf_op jit(solution)/shard_map/while/body/eval_jaxpr/gather | solution.py:67
  260.9 2.2 fusion.64
  263.8 6.6 %fusion.66 = f32[6,128,256]{2,0,1:T(8,128)} fusion(f32[24,128,256]{2,1,0:T(8,128)} %fusion.64, f32[6,128,256]{2,0,1:T(8,128)} %get-tuple-element.271, pred[]{:T(512)S(6)} %compare.4, f32[24]{0:T(128)S(1)} %fusion.65, s32[24]{0:T(128)S(1)} %gather_fusion.3), kind=kOutput, calls=%fused_computation.7.clone.1 | convolution fusion | flops 57016608 | bytes 4718785 | tf_op jit(solution)/shard_map/while/body/eval_jaxpr/sr,sif->rif/dot_general | solution.py:72
  272.9 3.5 %gather_fusion = bf16[24,128,128]{2,1,0:T(8,128)(2,1)S(1)} fusion(bf16[192,128,128]{2,1,0:T(8,128)(2,1)} %get-tuple-element.287, s32[1024]{0:T(1024)S(1)} %pad_clamp_fusion.4), kind=kCustom, calls=%fused_computation.1.clone.clone.1 | custom fusion | bytes 1572960 | tf_op jit(solution)/shard_map/while/body/eval_jaxpr/gather | solution.py:67
  276.4 2.2 fusion.64
  279.3 6.6 %fusion.66 = f32[6,128,256]{2,0,1:T(8,128)} fusion(f32[24,128,256]{2,1,0:T(8,128)} %fusion.64, f32[6,128,256]{2,0,1:T(8,128)} %get-tuple-element.271, pred[]{:T(512)S(6)} %compare.4, f32[24]{0:T(128)S(1)} %fusion.65, s32[24]{0:T(128)S(1)} %gather_fusion.3), kind=kOutput, calls=%fused_computation.7.clone.1 | convolution fusion | flops 57016608 | bytes 4718785 | tf_op jit(solution)/shard_map/while/body/eval_jaxpr/sr,sif->rif/dot_general | solution.py:72
  285.9 1.1 constant_dynamic-slice_fusion.4
  288.4 3.5 %gather_fusion = bf16[24,128,128]{2,1,0:T(8,128)(2,1)S(1)} fusion(bf16[192,128,128]{2,1,0:T(8,128)(2,1)} %get-tuple-element.287, s32[1024]{0:T(1024)S(1)} %pad_clamp_fusion.4), kind=kCustom, calls=%fused_computation.1.clone.clone.1 | custom fusion | bytes 1572960 | tf_op jit(solution)/shard_map/while/body/eval_jaxpr/gather | solution.py:67
  291.9 2.2 fusion.64
  294.8 6.6 %fusion.66 = f32[6,128,256]{2,0,1:T(8,128)} fusion(f32[24,128,256]{2,1,0:T(8,128)} %fusion.64, f32[6,128,256]{2,0,1:T(8,128)} %get-tuple-element.271, pred[]{:T(512)S(6)} %compare.4, f32[24]{0:T(128)S(1)} %fusion.65, s32[24]{0:T(128)S(1)} %gather_fusion.3), kind=kOutput, calls=%fused_computation.7.clone.1 | convolution fusion | flops 57016608 | bytes 4718785 | tf_op jit(solution)/shard_map/while/body/eval_jaxpr/sr,sif->rif/dot_general | solution.py:72
  301.4 1.1 constant_dynamic-slice_fusion.4
  303.9 3.5 %gather_fusion = bf16[24,128,128]{2,1,0:T(8,128)(2,1)S(1)} fusion(bf16[192,128,128]{2,1,0:T(8,128)(2,1)} %get-tuple-element.287, s32[1024]{0:T(1024)S(1)} %pad_clamp_fusion.4), kind=kCustom, calls=%fused_computation.1.clone.clone.1 | custom fusion | bytes 1572960 | tf_op jit(solution)/shard_map/while/body/eval_jaxpr/gather | solution.py:67
  307.4 2.2 fusion.64
  310.3 6.6 %fusion.66 = f32[6,128,256]{2,0,1:T(8,128)} fusion(f32[24,128,256]{2,1,0:T(8,128)} %fusion.64, f32[6,128,256]{2,0,1:T(8,128)} %get-tuple-element.271, pred[]{:T(512)S(6)} %compare.4, f32[24]{0:T(128)S(1)} %fusion.65, s32[24]{0:T(128)S(1)} %gather_fusion.3), kind=kOutput, calls=%fused_computation.7.clone.1 | convolution fusion | flops 57016608 | bytes 4718785 | tf_op jit(solution)/shard_map/while/body/eval_jaxpr/sr,sif->rif/dot_general | solution.py:72
  316.9 1.5 copy.52
  318.6 1.4 multiply_reduce_fusion
  320.2 2.1 multiply_reduce_fusion.1
  322.3 5.0 %fusion.23 = f32[768,2048]{1,0:T(8,128)} fusion(bf16[256,2048]{1,0:T(8,128)(2,1)} %all-gather.7.cloned.1.call-done, f32[768,256]{0,1:T(8,128)S(1)} %get-tuple-element.208, f32[256]{0:T(256)S(1)} %copy-done.3, f32[768]{0:T(1024)S(1)} %add_rsqrt_fusion), kind=kOutput, calls=%fused_computation.41 | convolution fusion | flops 805896192 | bytes 8130560 | tf_op jit(solution)/shard_map/dot_general | solution.py:82
  327.3 5.8 %fusion.22 = bf16[768,256]{0,1:T(8,128)(2,1)S(1)} fusion(f32[768,256]{0,1:T(8,128)S(1)} %get-tuple-element.208, bf16[256,2048]{1,0:T(8,128)(2,1)} %all-gather.11.cloned.1.call-done, f32[768,2048]{1,0:T(8,128)} %fusion.23, bf16[256,2048]{1,0:T(8,128)(2,1)} %all-gather.9.cloned.1.call-done, f32[256]{0:T(256)S(1)} %copy-done.3, f32[768]{0:T(1024)S(1)} %add_rsqrt_fusion), kind=kOutput, calls=%fused_computation.34 | convolution fusion | flops 1621032960 | bytes 9572352 | tf_op jit(solution)/shard_map/dot_general | solution.py:93
  (175 shorter events, 49.9 us)
Async XLA Ops:
  6.5 313.6 %copy-start = (bf16[1024,256]{1,0:T(8,128)(2,1)S(1)}, bf16[1024,256]{1,0:T(8,128)(2,1)}, u32[]{:S(2)}) copy-start(bf16[1024,256]{1,0:T(8,128)(2,1)} %param.23) | copy-start | bytes 1572868
  6.5 62.7 %all-gather.5.cloned.1.call-start = ((), (), s32[]{:S(2)}) async-start(), calls=%async_computation | async-start | bytes 8912896 | tf_op jit(solution)/shard_map/all_gather | solution.py:57
  7.3 315.0 %all-gather.7.cloned.1.call-start = ((), (), s32[]{:S(2)}) async-start(), calls=%async_computation.1 | async-start | bytes 1114112 | tf_op jit(solution)/shard_map/all_gather | solution.py:84
  8.0 319.3 %all-gather.11.cloned.1.call-start = ((), (), s32[]{:S(2)}) async-start(), calls=%async_computation.3 | async-start | bytes 1114112 | tf_op jit(solution)/shard_map/all_gather | solution.py:95
  8.7 318.6 %all-gather.9.cloned.1.call-start = ((), (), s32[]{:S(2)}) async-start(), calls=%async_computation.2 | async-start | bytes 1114112 | tf_op jit(solution)/shard_map/all_gather | solution.py:89
  13.0 56.3 %copy-start.1 = (s32[192]{0:T(256)S(1)}, s32[192]{0:T(256)}, u32[]{:S(2)}) copy-start(s32[192]{0:T(256)} %param.19) | copy-start | bytes 2308
  13.0 56.3 %copy-start.2 = (s32[192]{0:T(256)S(1)}, s32[192]{0:T(256)}, u32[]{:S(2)}) copy-start(s32[192]{0:T(256)} %param.20) | copy-start | bytes 2308
  69.2 250.9 %copy-start.4 = (f32[256]{0:T(256)S(1)}, f32[256]{0:T(256)}, u32[]{:S(2)}) copy-start(f32[256]{0:T(256)} %param.21) | copy-start | bytes 3076
  316.9 5.4 %copy-start.3 = (f32[256]{0:T(256)S(1)}, f32[256]{0:T(256)}, u32[]{:S(2)}) copy-start(f32[256]{0:T(256)} %param.24) | copy-start | bytes 3076
Sparse Core Ops, SparseCore 0:
  9.2 60.0 all-gather.4
  70.9 55.6 all-gather.6
  128.3 68.4 all-gather.10
  198.4 68.3 all-gather.8
where the time goes:
time: 342 us; the launch traced here: 341 us
  matrix products  153 us (45%)
  local copies, waits for them, and re-layouts  109 us (32%)
  waiting for transfers between devices  51.9 us (15%)
  between operations  13.2 us (4%)
  other arithmetic  12.4 us (4%)
    dot_general x16, matrix products, one_block(): jnp.einsum('sr,sif->rif', onehot, contrib, precision=lax.Precision.HIGHEST)  105 us
    gather x16, local copies, waits for them, and re-layouts, one_block(): masked[chosen]  55.8 us
    all_gather x1, waiting for transfers between devices, local(): source_piece = lax.all_gather(features, 'blk', axis=0, tiled=True)  49.2 us
    dot_general x16, matrix products, one_block(): jnp.einsum('sij,sjf->sif', masked[chosen], picked, preferred_element_type...  34.9 us
    gather x32, local copies, waits for them, and re-layouts, one_block(): picked = source_tiles[tile_col[chosen]]  21.7 us
    dynamic_slice x16, local copies, waits for them, and re-layouts, one_block(): lax.dynamic_slice_in_dim(source_piece, block_step * SRC_BLOCK, SRC_BLOCK, 0)  17.2 us
    gather x16, local copies, waits for them, and re-layouts, one_block(): tile_row[chosen][:, None] == row_ids[None, :]  11.3 us
    select_n x1, other arithmetic, local(): jnp.where(columns[None, None, :] < tile_limit[:, :, None], tile_weight, j...  7.02 us
  transfers between devices with their start and end apart: 4, of which 1 were waited for; matrix products, arithmetic and copies ran while one was open for 79% of the time, Pallas kernels for 0%

commit v1 on v0

--- a/solution.py
+++ b/solution.py
@@ -1,3 +1,4 @@
+import functools
 import jax
 import jax.numpy as jnp
 from jax import lax
@@ -9,6 +10,16 @@
 DEST_DEV = 768
 TILE_COUNT = 192
 SLOT_CAP = 24
+
+
+def do_quotas(message, named_axis):
+    return jnp.concatenate(
+        lax.all_to_all(jnp.stack(lax.axis_size(named_axis) * [message], axis=0), named_axis, 0, 0),
+        axis=0,
+    )
+
+
+group_shelves_up = functools.partial(do_quotas, named_axis="blk")
 
 
 def rms_scaled(values, norm_gain):
@@ -54,7 +65,7 @@
     slot_tile = jnp.sum(slot_match * tile_ids[:, None, None], axis=0)
     slot_live = jnp.sum(slot_match, axis=0).astype(jnp.float32)
     zero_rows = jnp.zeros((row_tiles, TILE_SIZE, FEATURES), jnp.float32)
-    source_piece = lax.all_gather(features, "blk", axis=0, tiled=True)
+    source_piece = group_shelves_up(features)
     block_count = source_piece.shape[0] // SRC_BLOCK
 
     def one_block(block_step, running):

time: 342 us -> 480 us (1.40)
  waiting for transfers between devices: 51.9 us -> 175 us
  starting transfers between devices: 0.12 us -> 10.2 us
  local copies, waits for them, and re-layouts: 109 us -> 114 us
    all_to_all x0 -> x1, waiting for transfers between devices: none -> 173 us  [do_quotas(): lax.all_to_all(jnp.stack(lax.axis_size(named_axis) * [message], axis=0),...]
    all_gather x1 -> x0, waiting for transfers between devices: 49.2 us -> none  [local(): source_piece = lax.all_gather(features, 'blk', axis=0, tiled=True)]
    all_to_all x0 -> x1, starting transfers between devices: none -> 10.1 us  [do_quotas(): lax.all_to_all(jnp.stack(lax.axis_size(named_axis) * [message], axis=0),...]
    another operation x1 -> x2, local copies, waits for them, and re-layouts: 0.01 us -> 5.12 us  [the longest x1 5.12 us: do_quotas(): jnp.stack(lax.axis_size(named_axis) * [message], axis=0)]
  transfers between devices with their start and end apart: 4 -> 4, of which waited for: 1 -> 1; matrix products, arithmetic and copies ran while one was open for 79% -> 56% of each run, Pallas kernels for 0% -> 0%
where the time goes in v1:
time: 480 us; the launch traced here: 479 us
  waiting for transfers between devices  175 us (36%)
  matrix products  155 us (32%)
  local copies, waits for them, and re-layouts  114 us (24%)
  between operations  13.3 us (3%)
  starting transfers between devices  10.2 us (2%)
  other arithmetic  10 us (2%)
    all_to_all x1, waiting for transfers between devices, do_quotas(): lax.all_to_all(jnp.stack(lax.axis_size(named_axis) * [message], axis=0),...  173 us
    dot_general x16, matrix products, one_block(): jnp.einsum('sr,sif->rif', onehot, contrib, precision=lax.Precision.HIGHEST)  105 us
    gather x16, local copies, waits for them, and re-layouts, one_block(): masked[chosen]  55.7 us
    dot_general x16, matrix products, one_block(): jnp.einsum('sij,sjf->sif', masked[chosen], picked, preferred_element_type...  37.1 us
    gather x32, local copies, waits for them, and re-layouts, one_block(): picked = source_tiles[tile_col[chosen]]  21.7 us
    dynamic_slice x16, local copies, waits for them, and re-layouts, one_block(): lax.dynamic_slice_in_dim(source_piece, block_step * SRC_BLOCK, SRC_BLOCK, 0)  17.2 us
    gather x16, local copies, waits for them, and re-layouts, one_block(): tile_row[chosen][:, None] == row_ids[None, :]  11.3 us
    all_to_all x1, starting transfers between devices, do_quotas(): lax.all_to_all(jnp.stack(lax.axis_size(named_axis) * [message], axis=0),...  10.1 us
  transfers between devices with their start and end apart: 4, of which 1 were waited for; matrix products, arithmetic and copies ran while one was open for 56% of the time, Pallas kernels for 0%

profile of v1, /device:TPU:1, one launch (start us, length us, event | category | flops | bytes accessed | tf_op | source)
XLA Modules:
  0.0 478.6 jit_solution(1566297172717445849)
XLA Ops:
  6.5 5.1 %stack.2 = bf16[16,1024,256]{2,1,0:T(8,128)(2,1)} broadcast(bf16[1024,256]{1,0:T(8,128)(2,1)} %param.15), dimensions={1,2} | broadcast | bytes 8912896 | tf_op jit(solution)/shard_map/stack | solution.py:17
  11.7 10.1 %all-to-all-start = ((bf16[16,1024,256]{2,1,0:T(8,128)(2,1)}), bf16[16,1024,256]{2,1,0:T(8,128)(2,1)}, u32[]{:S(2)}, u32[]{:S(2)}) async-start(bf16[16,1024,256]{2,1,0:T(8,128)(2,1)} %stack.2), calls=%async_computation | async-start | bytes 16777216 | tf_op jit(solution)/shard_map/all_to_all | solution.py:17
  25.6 6.7 %fusion.17 = bf16[192,128,128]{2,1,0:T(8,128)(2,1)} fusion(bf16[192,128,128]{2,1,0:T(8,128)(2,1)} %param.16, s32[192,128]{1,0:T(8,128)S(1)} %copy-done.3), kind=kLoop, calls=%fused_computation.27 | loop fusion | flops 6291456 | bytes 12681216 | tf_op jit(solution)/shard_map/jit(_where)/select_n | solution.py:49
  32.3 172.8 %all-to-all-done = bf16[16,1024,256]{2,1,0:T(8,128)(2,1)} async-done(((bf16[16,1024,256]{2,1,0:T(8,128)(2,1)}), bf16[16,1024,256]{2,1,0:T(8,128)(2,1)}, u32[]{:S(2)}, u32[]{:S(2)}) %all-to-all-start) | async-done | bytes 8388640 | tf_op jit(solution)/shard_map/all_to_all | solution.py:17
  205.2 249.7 %while.14 = (s32[]{:T(128)}, f32[6,128,256]{2,0,1:T(8,128)}, s32[16,24]{1,0:T(8,128)S(1)}, s32[192]{0:T(256)S(1)}, f32[16,24]{1,0:T(8,128)S(1)}, /*index=5*/bf16...) while((s32[]{:T(128)}, f32[6,128,256]{2,0,1:T(8,128)}, ...), condition=%wide.region_6.7_spmd.clone, body=%wide.region_5.6_spmd.clone.sunk | while | flops 258345392 | bytes 16000889 | solution.py:85
  205.2 1.1 constant_dynamic-slice_fusion.4
  207.7 3.5 gather_fusion
  211.2 2.3 fusion.64
  214.2 6.3 %fusion.66 = f32[6,128,256]{2,0,1:T(8,128)} fusion(f32[24,128,256]{2,1,0:T(8,128)} %fusion.64, f32[6,128,256]{2,0,1:T(8,128)} %get-tuple-element.271, pred[]{:T(512)S(6)} %compare.4, f32[24]{0:T(128)S(1)} %fusion.65, s32[24]{0:T(128)S(1)} %gather_fusion.3), kind=kOutput, calls=%fused_computation.7.clone.1 | convolution fusion | flops 57016608 | bytes 4718785 | tf_op jit(solution)/shard_map/while/body/eval_jaxpr/sr,sif->rif/dot_general | solution.py:83
  220.5 1.1 constant_dynamic-slice_fusion.4
  223.0 3.5 gather_fusion
  226.5 2.3 fusion.64
  229.5 6.6 %fusion.66 = f32[6,128,256]{2,0,1:T(8,128)} fusion(f32[24,128,256]{2,1,0:T(8,128)} %fusion.64, f32[6,128,256]{2,0,1:T(8,128)} %get-tuple-element.271, pred[]{:T(512)S(6)} %compare.4, f32[24]{0:T(128)S(1)} %fusion.65, s32[24]{0:T(128)S(1)} %gather_fusion.3), kind=kOutput, calls=%fused_computation.7.clone.1 | convolution fusion | flops 57016608 | bytes 4718785 | tf_op jit(solution)/shard_map/while/body/eval_jaxpr/sr,sif->rif/dot_general | solution.py:83
  236.1 1.1 constant_dynamic-slice_fusion.4
  238.6 3.5 gather_fusion
  242.1 2.3 fusion.64
  245.2 6.6 %fusion.66 = f32[6,128,256]{2,0,1:T(8,128)} fusion(f32[24,128,256]{2,1,0:T(8,128)} %fusion.64, f32[6,128,256]{2,0,1:T(8,128)} %get-tuple-element.271, pred[]{:T(512)S(6)} %compare.4, f32[24]{0:T(128)S(1)} %fusion.65, s32[24]{0:T(128)S(1)} %gather_fusion.3), kind=kOutput, calls=%fused_computation.7.clone.1 | convolution fusion | flops 57016608 | bytes 4718785 | tf_op jit(solution)/shard_map/while/body/eval_jaxpr/sr,sif->rif/dot_general | solution.py:83
  251.8 1.1 constant_dynamic-slice_fusion.4
  254.2 3.5 gather_fusion
  257.7 2.3 fusion.64
  260.8 6.6 %fusion.66 = f32[6,128,256]{2,0,1:T(8,128)} fusion(f32[24,128,256]{2,1,0:T(8,128)} %fusion.64, f32[6,128,256]{2,0,1:T(8,128)} %get-tuple-element.271, pred[]{:T(512)S(6)} %compare.4, f32[24]{0:T(128)S(1)} %fusion.65, s32[24]{0:T(128)S(1)} %gather_fusion.3), kind=kOutput, calls=%fused_computation.7.clone.1 | convolution fusion | flops 57016608 | bytes 4718785 | tf_op jit(solution)/shard_map/while/body/eval_jaxpr/sr,sif->rif/dot_general | solution.py:83
  267.4 1.1 constant_dynamic-slice_fusion.4
  269.9 3.5 gather_fusion
  273.4 2.3 fusion.64
  276.4 6.6 %fusion.66 = f32[6,128,256]{2,0,1:T(8,128)} fusion(f32[24,128,256]{2,1,0:T(8,128)} %fusion.64, f32[6,128,256]{2,0,1:T(8,128)} %get-tuple-element.271, pred[]{:T(512)S(6)} %compare.4, f32[24]{0:T(128)S(1)} %fusion.65, s32[24]{0:T(128)S(1)} %gather_fusion.3), kind=kOutput, calls=%fused_computation.7.clone.1 | convolution fusion | flops 57016608 | bytes 4718785 | tf_op jit(solution)/shard_map/while/body/eval_jaxpr/sr,sif->rif/dot_general | solution.py:83
  285.5 3.5 gather_fusion
  289.0 2.3 fusion.64
  292.0 6.6 %fusion.66 = f32[6,128,256]{2,0,1:T(8,128)} fusion(f32[24,128,256]{2,1,0:T(8,128)} %fusion.64, f32[6,128,256]{2,0,1:T(8,128)} %get-tuple-element.271, pred[]{:T(512)S(6)} %compare.4, f32[24]{0:T(128)S(1)} %fusion.65, s32[24]{0:T(128)S(1)} %gather_fusion.3), kind=kOutput, calls=%fused_computation.7.clone.1 | convolution fusion | flops 57016608 | bytes 4718785 | tf_op jit(solution)/shard_map/while/body/eval_jaxpr/sr,sif->rif/dot_general | solution.py:83
  301.1 3.5 gather_fusion
  304.6 2.3 fusion.64
  307.6 6.6 %fusion.66 = f32[6,128,256]{2,0,1:T(8,128)} fusion(f32[24,128,256]{2,1,0:T(8,128)} %fusion.64, f32[6,128,256]{2,0,1:T(8,128)} %get-tuple-element.271, pred[]{:T(512)S(6)} %compare.4, f32[24]{0:T(128)S(1)} %fusion.65, s32[24]{0:T(128)S(1)} %gather_fusion.3), kind=kOutput, calls=%fused_computation.7.clone.1 | convolution fusion | flops 57016608 | bytes 4718785 | tf_op jit(solution)/shard_map/while/body/eval_jaxpr/sr,sif->rif/dot_general | solution.py:83
  316.7 3.5 gather_fusion
  320.2 2.3 fusion.64
  323.3 6.6 %fusion.66 = f32[6,128,256]{2,0,1:T(8,128)} fusion(f32[24,128,256]{2,1,0:T(8,128)} %fusion.64, f32[6,128,256]{2,0,1:T(8,128)} %get-tuple-element.271, pred[]{:T(512)S(6)} %compare.4, f32[24]{0:T(128)S(1)} %fusion.65, s32[24]{0:T(128)S(1)} %gather_fusion.3), kind=kOutput, calls=%fused_computation.7.clone.1 | convolution fusion | flops 57016608 | bytes 4718785 | tf_op jit(solution)/shard_map/while/body/eval_jaxpr/sr,sif->rif/dot_general | solution.py:83
  329.9 1.1 constant_dynamic-slice_fusion.4
  332.4 3.5 gather_fusion
  335.8 2.3 fusion.64
  338.9 6.6 %fusion.66 = f32[6,128,256]{2,0,1:T(8,128)} fusion(f32[24,128,256]{2,1,0:T(8,128)} %fusion.64, f32[6,128,256]{2,0,1:T(8,128)} %get-tuple-element.271, pred[]{:T(512)S(6)} %compare.4, f32[24]{0:T(128)S(1)} %fusion.65, s32[24]{0:T(128)S(1)} %gather_fusion.3), kind=kOutput, calls=%fused_computation.7.clone.1 | convolution fusion | flops 57016608 | bytes 4718785 | tf_op jit(solution)/shard_map/while/body/eval_jaxpr/sr,sif->rif/dot_general | solution.py:83
  348.0 3.5 gather_fusion
  351.5 2.3 fusion.64
  354.5 6.6 %fusion.66 = f32[6,128,256]{2,0,1:T(8,128)} fusion(f32[24,128,256]{2,1,0:T(8,128)} %fusion.64, f32[6,128,256]{2,0,1:T(8,128)} %get-tuple-element.271, pred[]{:T(512)S(6)} %compare.4, f32[24]{0:T(128)S(1)} %fusion.65, s32[24]{0:T(128)S(1)} %gather_fusion.3), kind=kOutput, calls=%fused_computation.7.clone.1 | convolution fusion | flops 57016608 | bytes 4718785 | tf_op jit(solution)/shard_map/while/body/eval_jaxpr/sr,sif->rif/dot_general | solution.py:83
  363.6 3.5 gather_fusion
  367.1 2.3 fusion.64
  370.1 6.6 %fusion.66 = f32[6,128,256]{2,0,1:T(8,128)} fusion(f32[24,128,256]{2,1,0:T(8,128)} %fusion.64, f32[6,128,256]{2,0,1:T(8,128)} %get-tuple-element.271, pred[]{:T(512)S(6)} %compare.4, f32[24]{0:T(128)S(1)} %fusion.65, s32[24]{0:T(128)S(1)} %gather_fusion.3), kind=kOutput, calls=%fused_computation.7.clone.1 | convolution fusion | flops 57016608 | bytes 4718785 | tf_op jit(solution)/shard_map/while/body/eval_jaxpr/sr,sif->rif/dot_general | solution.py:83
  379.2 3.5 gather_fusion
  382.7 2.3 fusion.64
  385.7 6.6 %fusion.66 = f32[6,128,256]{2,0,1:T(8,128)} fusion(f32[24,128,256]{2,1,0:T(8,128)} %fusion.64, f32[6,128,256]{2,0,1:T(8,128)} %get-tuple-element.271, pred[]{:T(512)S(6)} %compare.4, f32[24]{0:T(128)S(1)} %fusion.65, s32[24]{0:T(128)S(1)} %gather_fusion.3), kind=kOutput, calls=%fused_computation.7.clone.1 | convolution fusion | flops 57016608 | bytes 4718785 | tf_op jit(solution)/shard_map/while/body/eval_jaxpr/sr,sif->rif/dot_general | solution.py:83
  394.8 3.5 gather_fusion
  398.3 2.3 fusion.64
  401.4 6.6 %fusion.66 = f32[6,128,256]{2,0,1:T(8,128)} fusion(f32[24,128,256]{2,1,0:T(8,128)} %fusion.64, f32[6,128,256]{2,0,1:T(8,128)} %get-tuple-element.271, pred[]{:T(512)S(6)} %compare.4, f32[24]{0:T(128)S(1)} %fusion.65, s32[24]{0:T(128)S(1)} %gather_fusion.3), kind=kOutput, calls=%fused_computation.7.clone.1 | convolution fusion | flops 57016608 | bytes 4718785 | tf_op jit(solution)/shard_map/while/body/eval_jaxpr/sr,sif->rif/dot_general | solution.py:83
  410.5 3.5 gather_fusion
  413.9 2.3 fusion.64
  417.0 6.6 %fusion.66 = f32[6,128,256]{2,0,1:T(8,128)} fusion(f32[24,128,256]{2,1,0:T(8,128)} %fusion.64, f32[6,128,256]{2,0,1:T(8,128)} %get-tuple-element.271, pred[]{:T(512)S(6)} %compare.4, f32[24]{0:T(128)S(1)} %fusion.65, s32[24]{0:T(128)S(1)} %gather_fusion.3), kind=kOutput, calls=%fused_computation.7.clone.1 | convolution fusion | flops 57016608 | bytes 4718785 | tf_op jit(solution)/shard_map/while/body/eval_jaxpr/sr,sif->rif/dot_general | solution.py:83
  426.1 3.5 gather_fusion
  429.6 2.3 fusion.64
  432.6 6.6 %fusion.66 = f32[6,128,256]{2,0,1:T(8,128)} fusion(f32[24,128,256]{2,1,0:T(8,128)} %fusion.64, f32[6,128,256]{2,0,1:T(8,128)} %get-tuple-element.271, pred[]{:T(512)S(6)} %compare.4, f32[24]{0:T(128)S(1)} %fusion.65, s32[24]{0:T(128)S(1)} %gather_fusion.3), kind=kOutput, calls=%fused_computation.7.clone.1 | convolution fusion | flops 57016608 | bytes 4718785 | tf_op jit(solution)/shard_map/while/body/eval_jaxpr/sr,sif->rif/dot_general | solution.py:83
  441.7 3.5 gather_fusion
  445.2 2.3 fusion.64
  448.2 6.6 %fusion.66 = f32[6,128,256]{2,0,1:T(8,128)} fusion(f32[24,128,256]{2,1,0:T(8,128)} %fusion.64, f32[6,128,256]{2,0,1:T(8,128)} %get-tuple-element.271, pred[]{:T(512)S(6)} %compare.4, f32[24]{0:T(128)S(1)} %fusion.65, s32[24]{0:T(128)S(1)} %gather_fusion.3), kind=kOutput, calls=%fused_computation.7.clone.1 | convolution fusion | flops 57016608 | bytes 4718785 | tf_op jit(solution)/shard_map/while/body/eval_jaxpr/sr,sif->rif/dot_general | solution.py:83
  454.8 1.5 copy.52
  456.6 1.4 multiply_reduce_fusion
  458.1 2.1 multiply_reduce_fusion.1
  460.3 5.0 %fusion.23 = f32[768,2048]{1,0:T(8,128)} fusion(bf16[256,2048]{1,0:T(8,128)(2,1)} %all-gather.4.cloned.1.call-done, f32[768,256]{0,1:T(8,128)S(1)} %get-tuple-element.208, f32[256]{0:T(256)S(1)} %copy-done.5, f32[768]{0:T(1024)S(1)} %add_rsqrt_fusion), kind=kOutput, calls=%fused_computation.41 | convolution fusion | flops 805896192 | bytes 8130560 | tf_op jit(solution)/shard_map/dot_general | solution.py:93
  465.3 5.8 %fusion.22 = bf16[768,256]{0,1:T(8,128)(2,1)S(1)} fusion(f32[768,256]{0,1:T(8,128)S(1)} %get-tuple-element.208, bf16[256,2048]{1,0:T(8,128)(2,1)} %all-gather.8.cloned.1.call-done, f32[768,2048]{1,0:T(8,128)} %fusion.23, bf16[256,2048]{1,0:T(8,128)(2,1)} %all-gather.6.cloned.1.call-done, f32[256]{0:T(256)S(1)} %copy-done.5, f32[768]{0:T(1024)S(1)} %add_rsqrt_fusion), kind=kOutput, calls=%fused_computation.34 | convolution fusion | flops 1621032960 | bytes 9572352 | tf_op jit(solution)/shard_map/dot_general | solution.py:104
  (179 shorter events, 49.5 us)
Async XLA Ops:
  6.5 451.6 %copy-start = (bf16[1024,256]{1,0:T(8,128)(2,1)S(1)}, bf16[1024,256]{1,0:T(8,128)(2,1)}, u32[]{:S(2)}) copy-start(bf16[1024,256]{1,0:T(8,128)(2,1)} %param.23) | copy-start | bytes 1572868
  11.7 12.3 %copy-start.4 = (s32[192,1]{0,1:T(1,128)S(1)}, s32[192,1]{0,1:T(1,128)}, u32[]{:S(2)}) copy-start(s32[192,1]{0,1:T(1,128)} %param.18) | copy-start | bytes 2308
  11.7 14.0 %copy-start.3 = (s32[192,128]{1,0:T(8,128)S(1)}, s32[192,128]{1,0:T(8,128)}, u32[]{:S(2)}) copy-start(s32[192,128]{1,0:T(8,128)} %param.17) | copy-start | bytes 294916
  11.7 193.5 %all-to-all-start = ((bf16[16,1024,256]{2,1,0:T(8,128)(2,1)}), bf16[16,1024,256]{2,1,0:T(8,128)(2,1)}, u32[]{:S(2)}, u32[]{:S(2)}) async-start(bf16[16,1024,256]{2,1,0:T(8,128)(2,1)} %stack.2), calls=%async_computation | async-start | bytes 16777216 | tf_op jit(solution)/shard_map/all_to_all | solution.py:17
  21.8 438.5 %all-gather.4.cloned.1.call-start = ((), (), s32[]{:S(2)}) async-start(), calls=%async_computation.1 | async-start | bytes 1114112 | tf_op jit(solution)/shard_map/all_gather | solution.py:95
  22.5 442.8 %all-gather.6.cloned.1.call-start = ((), (), s32[]{:S(2)}) async-start(), calls=%async_computation.2 | async-start | bytes 1114112 | tf_op jit(solution)/shard_map/all_gather | solution.py:100
  23.2 442.0 %all-gather.8.cloned.1.call-start = ((), (), s32[]{:S(2)}) async-start(), calls=%async_computation.3 | async-start | bytes 1114112 | tf_op jit(solution)/shard_map/all_gather | solution.py:106
  25.6 179.5 %copy-start.1 = (s32[192]{0:T(256)S(1)}, s32[192]{0:T(256)}, u32[]{:S(2)}) copy-start(s32[192]{0:T(256)} %param.19) | copy-start | bytes 2308
  25.6 179.5 %copy-start.2 = (s32[192]{0:T(256)S(1)}, s32[192]{0:T(256)}, u32[]{:S(2)}) copy-start(s32[192]{0:T(256)} %param.20) | copy-start | bytes 2308
  205.2 253.0 %copy-start.6 = (f32[256]{0:T(256)S(1)}, f32[256]{0:T(256)}, u32[]{:S(2)}) copy-start(f32[256]{0:T(256)} %param.21) | copy-start | bytes 3076
  454.8 5.4 %copy-start.5 = (f32[256]{0:T(256)S(1)}, f32[256]{0:T(256)}, u32[]{:S(2)}) copy-start(f32[256]{0:T(256)} %param.24) | copy-start | bytes 3076
Sparse Core Ops, SparseCore 0:
  24.3 58.7 all-gather.3
  84.8 67.4 all-gather.5
  154.0 68.4 all-gather.7
